TPU v7x, 32 devices: a whole 2x2x4 slice. The times are simulated.
32 devices in a mesh: gz: 4 (over y, x), gy: 2 (over core), gx: 4 (over z).
Axes of the slice: x: 2, y: 2, z: 4, core: 2. Of those that a mesh axis runs over, the one named last changes fastest.
Arguments:
- populations: float32 [19, 32, 16, 512], P(None, 'gz', 'gy', 'gx'), may hold values from 0.1 to 20, as said below
- solid: int32 [32, 16, 512], P('gz', 'gy', 'gx'), may hold values 0 or 1
- ports: int32 [2, 16, 512], P(None, 'gy', 'gx'), may hold values 0 or 1
- concentration: float32 [2, 4, 2, 64], P(None, 'gz'), may hold values from 0 to 1
- loaded: float32 [2, 4, 2, 64], P(None, 'gz'), may hold values from 0 to 2
Outputs:
- final_populations: float32 [19, 32, 16, 512], P(None, 'gz', 'gy', 'gx')
- new_concentration: float32 [2, 4, 2, 64], P(None, 'gz')
- new_loaded: float32 [2, 4, 2, 64], P(None, 'gz')
Inputs may be any that keep to these rules, and one draw needn't show every extreme that they name: `populations`: every population is positive and of the size of its lattice weight times 36.
All inputs are finite; a program needn't handle non-finite values. No bound on the sum of `solid` or of `ports` on one device may be relied on, other than what follows from the above.
Results may differ from a plain program's by a relative error of at most 0.00002.
Values sent between devices are 32-bit elements; how exact they have to be, the bound alone decides.
A program may use at most 64 MiB of HBM per device.

v0:
```python
import jax
import jax.numpy as jnp
from jax import lax
from jax.sharding import PartitionSpec as P

ITERS = 2
lattice = [
    (0, 0, 0),
    (1, 0, 0),
    (-1, 0, 0),
    (0, 1, 0),
    (0, -1, 0),
    (0, 0, 1),
    (0, 0, -1),
    (1, 1, 0),
    (-1, -1, 0),
    (1, -1, 0),
    (-1, 1, 0),
    (1, 0, 1),
    (-1, 0, -1),
    (1, 0, -1),
    (-1, 0, 1),
    (0, 1, 1),
    (0, -1, -1),
    (0, 1, -1),
    (0, -1, 1),
]
opposite = [0, 2, 1, 4, 3, 6, 5, 8, 7, 10, 9, 12, 11, 14, 13, 16, 15, 18, 17]
weights = [1.0 / 3.0] + [1.0 / 18.0] * 6 + [1.0 / 36.0] * 12
relax_rate = 1.25
base_density = 36.0
inlet_speed = 0.05
spread_base = (0.03, 0.06)
spread_length = 0.1
uptake_rate = (0.3, 0.6)
affinity = (2.0, 0.5)
phase_ratio = 0.5
feed_level = (1.0, 0.5)


def extended(cells, sides, width, closed):
    for axis, dim in sides:
        count = lax.axis_size(axis)
        ends = count if closed else count - 1
        head = lax.slice_in_dim(cells, 0, width, axis=dim)
        tail = lax.slice_in_dim(cells, cells.shape[dim] - width, cells.shape[dim], axis=dim)
        cells = jnp.concatenate(
            [
                lax.ppermute(tail, axis, [(i, (i + 1) % count) for i in range(ends)]),
                cells,
                lax.ppermute(head, axis, [((i + 1) % count, i) for i in range(ends)]),
            ],
            axis=dim,
        )
    return cells


def equilibrium(density, velocity):
    speed_z, speed_y, speed_x = velocity
    square = speed_z * speed_z + speed_y * speed_y + speed_x * speed_x
    result = []
    for member in range(19):
        step_z, step_y, step_x = lattice[member]
        along = step_z * speed_z + step_y * speed_y + step_x * speed_x
        result.append(
            weights[member] * density * (1.0 + 3.0 * along + 4.5 * along * along - 1.5 * square)
        )
    return result


def moments(pops):
    density = pops[0]
    for member in range(1, 19):
        density = density + pops[member]
    flows = []
    for position in range(3):
        total = jnp.zeros_like(pops[0])
        for member in range(19):
            heading = lattice[member][position]
            if heading == 1:
                total = total + pops[member]
            elif heading == -1:
                total = total - pops[member]
        flows.append(total)
    return (density, flows)


def collide(pops, solid_flag):
    density, flows = moments(pops)
    velocity = [flow / density for flow in flows]
    balance = equilibrium(density, velocity)
    post = [
        jnp.where(
            solid_flag,
            pops[opposite[member]],
            pops[member] - relax_rate * (pops[member] - balance[member]),
        )
        for member in range(19)
    ]
    return (post, velocity)


def close_ends(moved, post, velocity, ports, first_dev, last_dev):
    inflow = equilibrium(base_density, (inlet_speed, 0.0, 0.0))
    outflow = equilibrium(base_density, (velocity[0][-1], velocity[1][-1], velocity[2][-1]))
    inlet_open = ports[0] == 1
    outlet_open = ports[1] == 1
    result = list(moved)
    for member in range(19):
        step_z = lattice[member][0]
        back = post[opposite[member]]
        if step_z == 1:
            entering = jnp.where(inlet_open, inflow[member], back[0])
            result[member] = (
                result[member].at[0].set(jnp.where(first_dev, entering, result[member][0]))
            )
        elif step_z == -1:
            entering = jnp.where(outlet_open, outflow[member], back[-1])
            result[member] = (
                result[member].at[-1].set(jnp.where(last_dev, entering, result[member][-1]))
            )
    return result


def block_sum(field):
    depth, height, width = field.shape
    return field.reshape(depth // 8, 8, height // 8, 8, width // 8, 8).sum(axis=(1, 3, 5))


def transport(padded, loaded, coarse_vel):
    centre = padded[:, 1:-1]
    neighbours = [
        (padded[:, :-2], padded[:, 2:]),
        (jnp.roll(centre, 1, axis=2), jnp.roll(centre, -1, axis=2)),
        (jnp.roll(centre, 1, axis=3), jnp.roll(centre, -1, axis=3)),
    ]
    change = jnp.zeros_like(centre)
    curvature = jnp.zeros_like(centre)
    reach = jnp.zeros_like(coarse_vel[0])
    for direction in range(3):
        courant = 8.0 * coarse_vel[direction]
        before, after = neighbours[direction]
        change = (
            change
            - jnp.maximum(courant, 0.0) * (centre - before)
            - jnp.minimum(courant, 0.0) * (after - centre)
        )
        curvature = curvature + after - 2.0 * centre + before
        reach = reach + jnp.abs(courant)
    base = jnp.array(spread_base, dtype=centre.dtype)[:, None, None, None]
    speed = jnp.array(uptake_rate, dtype=centre.dtype)[:, None, None, None]
    holding = jnp.array(affinity, dtype=centre.dtype)[:, None, None, None]
    rate = speed * (holding * centre - loaded)
    new_conc = centre + change + (base + spread_length * reach) * curvature - phase_ratio * rate
    return (new_conc, loaded + rate)


def body(populations, solid, ports, concentration, loaded):
    depth, height, width = solid.shape
    slab_pos = lax.axis_index("gz")
    first_dev = slab_pos == 0
    last_dev = slab_pos == lax.axis_size("gz") - 1
    pops = [populations[member] for member in range(19)]
    solid_flag = solid == 1
    for iteration in range(ITERS):
        post, velocity = collide(pops, solid_flag)
        padded = extended(jnp.stack(post), (("gz", 1), ("gy", 2), ("gx", 3)), 1, True)
        moved = []
        for member in range(19):
            step_z, step_y, step_x = lattice[member]
            moved.append(
                padded[
                    member,
                    1 - step_z : 1 - step_z + depth,
                    1 - step_y : 1 - step_y + height,
                    1 - step_x : 1 - step_x + width,
                ]
            )
        pops = close_ends(moved, post, velocity, ports, first_dev, last_dev)
    final = jnp.stack(pops)
    density, flows = moments(pops)
    fluid = (solid == 0).astype(jnp.float32)
    local = jnp.stack([block_sum(flow * fluid) for flow in flows]) / (512.0 * base_density)
    across = lax.all_gather(local, "gy", axis=2, tiled=True)
    coarse_vel = lax.all_gather(across, "gx", axis=3, tiled=True)
    padded_conc = extended(concentration, (("gz", 1),), 1, False)
    feed = jnp.broadcast_to(
        jnp.array(feed_level, dtype=jnp.float32)[:, None, None],
        (2, concentration.shape[2], concentration.shape[3]),
    )
    front = jnp.where(first_dev, feed, padded_conc[:, 0])
    rear = jnp.where(last_dev, concentration[:, -1], padded_conc[:, -1])
    padded_conc = padded_conc.at[:, 0].set(front).at[:, -1].set(rear)
    new_conc, new_load = transport(padded_conc, loaded, coarse_vel)
    return (final, new_conc, new_load)


def solution(mesh):
    placed = (
        P(None, "gz", "gy", "gx"),
        P("gz", "gy", "gx"),
        P(None, "gy", "gx"),
        P(None, "gz", None, None),
        P(None, "gz", None, None),
    )
    return jax.shard_map(
        body,
        mesh=mesh,
        in_specs=placed,
        out_specs=(P(None, "gz", "gy", "gx"), P(None, "gz", None, None), P(None, "gz", None, None)),
        check_vma=False,
    )
```

profile of v0, /device:TPU:0, one launch (start us, length us, event | category | flops | bytes accessed | tf_op | source)
XLA Modules:
  0.0 104.6 jit_solution(4216951791328130897)
XLA Ops:
  0.6 5.6 %collective-permute-start.12 = (f32[2,1,2,64]{3,2,1,0:T(2,128)}, f32[2,1,2,64]{3,2,1,0:T(2,128)}, u32[]{:S(2)}, u32[]{:S(2)}) collective-permute-start(f32[2,1,2,64]{3,2,1,0:T(2,128)} %param.56), channel_id=1, source_target_pairs={{0,8},{8,16},{16,24},{1,9},{9,17},{17,25},{2,10},{10,18},{18,26},{... | collective-permute-start | bytes 3080 | tf_op jit(solution)/shard_map/ppermute | solution.py:49
  6.2 1.3 %collective-permute-start.13 = (f32[2,1,2,64]{3,2,1,0:T(2,128)}, f32[2,1,2,64]{3,2,1,0:T(2,128)}, u32[]{:S(2)}, u32[]{:S(2)}) collective-permute-start(f32[2,1,2,64]{3,2,1,0:T(2,128)} %param.56), channel_id=1, source_target_pairs={{8,0},{16,8},{24,16},{9,1},{17,9},{25,17},{10,2},{18,10},{26,18},{... | collective-permute-start | bytes 3080 | tf_op jit(solution)/shard_map/ppermute | solution.py:51
  7.5 1.2 %constant_dynamic-update-slice_fusion.18 = (f32[19,8,8,128]{3,2,1,0:T(8,128)S(1)}, f32[8,8,128]{2,1,0:T(8,128)S(1)}, f32[8,8,128]{2,1,0:T(8,128)S(1)}, f32[8,8,1...) fusion(f32[19,8,8,128]{3,2,1,0:T(8,128)} %param.53, ...), kind=kLoop, calls=%fused_computation.20 | loop fusion | flops 589823 | bytes 860160
  8.7 0.8 constant_dynamic-update-slice_fusion.17
  9.5 0.8 constant_dynamic-update-slice_fusion.16
  10.3 0.8 constant_dynamic-update-slice_fusion.15
  11.8 2.7 %collective-permute-start = (f32[19,1,8,128]{3,2,1,0:T(8,128)S(1)}, f32[19,1,8,128]{3,2,1,0:T(8,128)S(1)}, u32[]{:S(2)}, u32[]{:S(2)}) collective-permute-start(f32[19,1,8,128]{3,2,1,0:T(8,128)S(1)} %get-tuple-element.383), channel_id=1, source_target_pairs={{0,8},{8,16},{16,24},{24,0},{1,9},{9,17},{17,25},{25,1},{2,10},{10... | collective-permute-start | bytes 233480 | tf_op jit(solution)/shard_map/ppermute | solution.py:49
  14.5 1.0 collective-permute-start.1
  16.2 2.4 %collective-permute-done = f32[19,1,8,128]{3,2,1,0:T(8,128)S(1)} collective-permute-done((f32[19,1,8,128]{3,2,1,0:T(8,128)S(1)}, f32[19,1,8,128]{3,2,1,0:T(8,128)S(1)}, u32[]{:S(2)}, u32[]{:S(2)}) %collective-permute-start) | collective-permute-done | bytes 77856 | tf_op jit(solution)/shard_map/ppermute | solution.py:49
  18.6 0.9 collective-permute-done.1
  21.5 1.7 %fusion.386 = (f32[19,10,10,1]{3,2,1,0:T(8,128)}, f32[19,10,10,1]{3,2,1,0:T(8,128)S(1)}) fusion(f32[19,10,10,128]{3,2,1,0:T(8,128)S(1)} %pad_maximum_fusion), kind=kLoop, calls=%fused_computation.679 | loop fusion | bytes 30400 | tf_op jit(solution)/shard_map/slice | solution.py:45
  23.2 2.1 %copy.55 = f32[19,10,10,1]{0,3,2,1:T(1,128)S(1)} copy(f32[19,10,10,1]{3,2,1,0:T(8,128)} %get-tuple-element.355) | data formatting | bytes 15200 | tf_op jit(solution)/shard_map/slice | solution.py:45
  25.4 3.6 %collective-permute-start.5 = (f32[19,10,10,1]{0,3,2,1:T(1,128)S(1)}, f32[19,10,10,1]{0,3,2,1:T(1,128)S(1)}, u32[]{:S(2)}, u32[]{:S(2)}) collective-permute-start(f32[19,10,10,1]{0,3,2,1:T(1,128)S(1)} %copy.55), channel_id=1, source_target_pairs={{1,0},{2,1},{3,2},{0,3},{5,4},{6,5},{7,6},{4,7},{9,8},{10,9},{11,1... | collective-permute-start | bytes 22808 | tf_op jit(solution)/shard_map/ppermute | solution.py:51
  29.0 0.8 copy.53
  29.9 1.1 %collective-permute-done.5 = f32[19,10,10,1]{0,3,2,1:T(1,128)S(1)} collective-permute-done((f32[19,10,10,1]{0,3,2,1:T(1,128)S(1)}, f32[19,10,10,1]{0,3,2,1:T(1,128)S(1)}, u32[]{:S(2)}, u32[]{:S(2)}) %collective-permute-start.5) | collective-permute-done | bytes 7632 | tf_op jit(solution)/shard_map/ppermute | solution.py:51
  31.0 1.6 %copy.56 = f32[19,10,10,1]{3,2,1,0:T(8,128)S(1)} copy(f32[19,10,10,1]{0,3,2,1:T(1,128)S(1)} %collective-permute-done.5) | data formatting | bytes 15200 | tf_op jit(solution)/shard_map/ppermute | solution.py:51
  32.7 3.0 %collective-permute-done.4 = f32[19,10,10,1]{0,3,2,1:T(1,128)S(1)} collective-permute-done((f32[19,10,10,1]{0,3,2,1:T(1,128)S(1)}, f32[19,10,10,1]{0,3,2,1:T(1,128)S(1)}, u32[]{:S(2)}, u32[]{:S(2)}) %collective-permute-start.4) | collective-permute-done | bytes 7632 | tf_op jit(solution)/shard_map/ppermute | solution.py:49
  35.7 2.7 %copy.54 = f32[19,10,10,1]{3,2,1,0:T(8,128)} copy(f32[19,10,10,1]{0,3,2,1:T(1,128)S(1)} %collective-permute-done.4) | data formatting | bytes 15200 | tf_op jit(solution)/shard_map/ppermute | solution.py:49
  38.4 1.0 maximum_bitcast_fusion.13
  39.5 1.3 %copy-done = f32[19,10,10,1]{3,2,1,0:T(8,128)S(1)} copy-done((f32[19,10,10,1]{3,2,1,0:T(8,128)S(1)}, f32[19,10,10,1]{3,2,1,0:T(8,128)}, u32[]{:S(2)}) %copy-start) | copy-done | bytes 7624
  48.5 2.1 %collective-permute-start.6 = (f32[19,1,8,128]{3,2,1,0:T(8,128)S(1)}, f32[19,1,8,128]{3,2,1,0:T(8,128)S(1)}, u32[]{:S(2)}, u32[]{:S(2)}) collective-permute-start(f32[19,1,8,128]{3,2,1,0:T(8,128)S(1)} %get-tuple-element.382), channel_id=1, source_target_pairs={{0,8},{8,16},{16,24},{24,0},{1,9},{9,17},{17,25},{25,1},{2,10},{10... | collective-permute-start | bytes 233480 | tf_op jit(solution)/shard_map/ppermute | solution.py:49
  50.6 0.8 collective-permute-start.7
  52.1 1.7 %collective-permute-done.6 = f32[19,1,8,128]{3,2,1,0:T(8,128)S(1)} collective-permute-done((f32[19,1,8,128]{3,2,1,0:T(8,128)S(1)}, f32[19,1,8,128]{3,2,1,0:T(8,128)S(1)}, u32[]{:S(2)}, u32[]{:S(2)}) %collective-permute-start.6) | collective-permute-done | bytes 77856 | tf_op jit(solution)/shard_map/ppermute | solution.py:49
  53.8 1.2 %collective-permute-done.7 = f32[19,1,8,128]{3,2,1,0:T(8,128)S(1)} collective-permute-done((f32[19,1,8,128]{3,2,1,0:T(8,128)S(1)}, f32[19,1,8,128]{3,2,1,0:T(8,128)S(1)}, u32[]{:S(2)}, u32[]{:S(2)}) %collective-permute-start.7) | collective-permute-done | bytes 77856 | tf_op jit(solution)/shard_map/ppermute | solution.py:51
  57.0 1.7 %fusion.385 = (f32[19,10,10,1]{3,2,1,0:T(8,128)S(1)}, f32[19,10,10,1]{3,2,1,0:T(8,128)}) fusion(f32[19,10,10,128]{3,2,1,0:T(8,128)S(1)} %pad_maximum_fusion.1), kind=kLoop, calls=%fused_computation.678 | loop fusion | bytes 30400 | tf_op jit(solution)/shard_map/slice | solution.py:45
  58.7 2.1 %copy.57 = f32[19,10,10,1]{0,3,2,1:T(1,128)S(1)} copy(f32[19,10,10,1]{3,2,1,0:T(8,128)} %get-tuple-element.354) | data formatting | bytes 15200 | tf_op jit(solution)/shard_map/slice | solution.py:46
  60.9 0.8 copy.59
  61.6 4.0 %collective-permute-start.11 = (f32[19,10,10,1]{0,3,2,1:T(1,128)S(1)}, f32[19,10,10,1]{0,3,2,1:T(1,128)}, u32[]{:S(2)}, u32[]{:S(2)}) collective-permute-start(f32[19,10,10,1]{0,3,2,1:T(1,128)S(1)} %copy.59), channel_id=1, source_target_pairs={{1,0},{2,1},{3,2},{0,3},{5,4},{6,5},{7,6},{4,7},{9,8},{10,9},{11,1... | collective-permute-start | bytes 22808 | tf_op jit(solution)/shard_map/ppermute | solution.py:51
  65.7 1.7 %collective-permute-done.11 = f32[19,10,10,1]{0,3,2,1:T(1,128)} collective-permute-done((f32[19,10,10,1]{0,3,2,1:T(1,128)S(1)}, f32[19,10,10,1]{0,3,2,1:T(1,128)}, u32[]{:S(2)}, u32[]{:S(2)}) %collective-permute-start.11) | collective-permute-done | bytes 7632 | tf_op jit(solution)/shard_map/ppermute | solution.py:51
  67.4 2.4 %copy.60 = f32[19,10,10,1]{3,2,1,0:T(8,128)S(1)} copy(f32[19,10,10,1]{0,3,2,1:T(1,128)} %collective-permute-done.11) | data formatting | bytes 15200 | tf_op jit(solution)/shard_map/ppermute | solution.py:51
  70.5 0.7 constant_dynamic-update-slice_fusion.64
  71.8 3.4 %copy.58 = f32[19,10,10,1]{3,2,1,0:T(8,128)} copy(f32[19,10,10,1]{0,3,2,1:T(1,128)} %collective-permute-done.10) | data formatting | bytes 15200 | tf_op jit(solution)/shard_map/ppermute | solution.py:49
  75.3 1.1 %maximum_bitcast_fusion.3 = (f32[8,8,128]{2,1,0:T(8,128)S(1)}, f32[8,8,128]{2,1,0:T(8,128)S(1)}, f32[8,8,128]{2,1,0:T(8,128)S(1)}) fusion(f32[19,10,10,1]{3,2,1,0:T(8,128)} %copy.58, f32[19,10,1,128]{3,2,1,0:T(1,128)S(1)} %collective-permute-done.9, f32[19,10,1,128]{3,2,1,0:T(1,128)S(1)} %collective-permute-done.8, ...), kind=kLoop, calls=%fused_computation.399 | loop fusion | flops 106496 | bytes 1078704 | tf_op jit(solution)/shard_map/squeeze | solution.py:172
  76.7 0.8 constant_dynamic-update-slice_fusion.57
  77.5 0.7 constant_dynamic-update-slice_fusion.61
  78.2 0.7 constant_dynamic-update-slice_fusion.59
  78.9 0.8 constant_dynamic-update-slice_fusion.60
  79.7 0.7 constant_dynamic-update-slice_fusion.63
  80.5 1.4 %select_reduce_fusion = (f32[128]{0:T(128)}, f32[128]{0:T(128)S(1)}, f32[128]{0:T(128)}, f32[1,8,8,128]{3,2,1,0:T(8,128)S(1)}, f32[1,8,8,128]{3,2,1,0:T(8,128)S(...) fusion(f32[8,8,128]{2,1,0:T(8,128)S(1)} %get-tuple-element.278,, ...), kind=kLoop, calls=%fused_computation.509 | loop fusion | flops 573056 | bytes 1612128 | tf_op jit(solution)/shard_map/reduce_sum | solution.py:127
  81.9 0.7 reduce_sum.37
  82.7 0.7 reduce_sum.40
  83.9 1.8 %all_gather.6 = f32[3,1,2,16]{3,1,0,2:T(1,128)S(1)} all-gather(f32[3,1,1,16]{3,1,0,2:T(1,128)S(1)} %fusion.358), channel_id=1, replica_groups=mesh['gz'=4,'gy'=2,'gx'=4] {'gy'}, dimensions={2}, use_global_device_ids=true | all-gather | bytes 576 | tf_op jit(solution)/shard_map/all_gather | solution.py:184
  85.8 13.6 %all_gather.7 = f32[3,1,2,64]{0,2,1,3:T(2,128)S(1)} all-gather(f32[3,1,2,16]{0,2,1,3:T(2,128)S(1)} %copy.62), channel_id=1, replica_groups=mesh['gz'=4,'gy'=2,'gx'=4] {'gx'}, dimensions={3}, use_global_device_ids=true | all-gather | bytes 1920 | tf_op jit(solution)/shard_map/all_gather | solution.py:185
  99.9 0.8 constant_dynamic-update-slice_fusion.53
  100.7 0.8 constant_dynamic-update-slice_fusion.52
  101.4 0.8 constant_dynamic-update-slice_fusion.51
  102.2 0.8 constant_dynamic-update-slice_fusion.50
  103.3 1.4 %multiply_subtract_fusion = f32[2,1,2,64]{3,2,1,0:T(2,128)} fusion(f32[2,1,2,64]{3,2,1,0:T(2,128)S(1)} %copy-done.9, f32[2,1,2,1]{3,2,1,0:T(2,128)S(1)} %copy-done.19, f32[2,1,2,63]{3,2,1,0:T(2,128)S(1)} %copy-done.21, f32[2,1,2,63]{3,2,1,0:T(2,128)S(1)} %copy-done.20, f32[2,1,2,1]{3,2,1,0:T(2,128)S(1)} %copy-done.18, f32[2,1,1,64]{3,2,1,0:T(1,128)S(1)} %copy-done.23, ...), kind=kLoop, calls=%fused_computation.666 | loop fusion | flops 10496 | bytes 11810 | tf_op jit(solution)/shard_map/sub | solution.py:154
  (154 shorter events, 16.6 us)
Async XLA Ops:
  0.6 10.5 %copy-start.2 = (f32[19,8,8,128]{3,2,1,0:T(8,128)S(1)}, f32[19,8,8,128]{3,2,1,0:T(8,128)}, u32[]{:S(2)}) copy-start(f32[19,8,8,128]{3,2,1,0:T(8,128)} %param.53) | copy-start | bytes 1867780
  0.6 102.5 %collective-permute-start.12 = (f32[2,1,2,64]{3,2,1,0:T(2,128)}, f32[2,1,2,64]{3,2,1,0:T(2,128)}, u32[]{:S(2)}, u32[]{:S(2)}) collective-permute-start(f32[2,1,2,64]{3,2,1,0:T(2,128)} %param.56), channel_id=1, source_target_pairs={{0,8},{8,16},{16,24},{1,9},{9,17},{17,25},{2,10},{10,18},{18,26},{... | collective-permute-start | bytes 3080 | tf_op jit(solution)/shard_map/ppermute | solution.py:49
  6.2 96.9 %collective-permute-start.13 = (f32[2,1,2,64]{3,2,1,0:T(2,128)}, f32[2,1,2,64]{3,2,1,0:T(2,128)}, u32[]{:S(2)}, u32[]{:S(2)}) collective-permute-start(f32[2,1,2,64]{3,2,1,0:T(2,128)} %param.56), channel_id=1, source_target_pairs={{8,0},{16,8},{24,16},{9,1},{17,9},{25,17},{10,2},{18,10},{26,18},{... | collective-permute-start | bytes 3080 | tf_op jit(solution)/shard_map/ppermute | solution.py:51
  11.3 4.3 %copy-start.8 = (f32[2,1,2,64]{3,2,1,0:T(2,128)S(1)}, f32[2,1,2,64]{3,2,1,0:T(2,128)}, u32[]{:S(2)}) copy-start(f32[2,1,2,64]{3,2,1,0:T(2,128)} %param.56) | copy-start | bytes 3076
  11.3 4.2 %copy-start.16 = (f32[2,1,2,64]{3,2,1,0:T(2,128)S(1)}, f32[2,1,2,64]{3,2,1,0:T(2,128)}, u32[]{:S(2)}) copy-start(f32[2,1,2,64]{3,2,1,0:T(2,128)} %param.57) | copy-start | bytes 3076
  11.3 4.2 %copy-start.24 = (f32[2]{0:T(128)S(1)}, f32[2]{0:T(128)}, u32[]{:S(2)}) copy-start(f32[2]{0:T(128)} %constant.557.clone) | copy-start | bytes 28
  11.3 4.2 %copy-start.26 = (f32[2]{0:T(128)S(1)}, f32[2]{0:T(128)}, u32[]{:S(2)}) copy-start(f32[2]{0:T(128)} %constant.558.clone) | copy-start | bytes 28
  11.8 6.8 %collective-permute-start = (f32[19,1,8,128]{3,2,1,0:T(8,128)S(1)}, f32[19,1,8,128]{3,2,1,0:T(8,128)S(1)}, u32[]{:S(2)}, u32[]{:S(2)}) collective-permute-start(f32[19,1,8,128]{3,2,1,0:T(8,128)S(1)} %get-tuple-element.383), channel_id=1, source_target_pairs={{0,8},{8,16},{16,24},{24,0},{1,9},{9,17},{17,25},{25,1},{2,10},{10... | collective-permute-start | bytes 233480 | tf_op jit(solution)/shard_map/ppermute | solution.py:49
  14.5 5.0 %collective-permute-start.1 = (f32[19,1,8,128]{3,2,1,0:T(8,128)S(1)}, f32[19,1,8,128]{3,2,1,0:T(8,128)S(1)}, u32[]{:S(2)}, u32[]{:S(2)}) collective-permute-start(f32[19,1,8,128]{3,2,1,0:T(8,128)S(1)} %get-tuple-element.384), channel_id=1, source_target_pairs={{8,0},{16,8},{24,16},{0,24},{9,1},{17,9},{25,17},{1,25},{10,2},{18... | collective-permute-start | bytes 233480 | tf_op jit(solution)/shard_map/ppermute | solution.py:51
  19.7 1.4 %collective-permute-start.2 = (f32[19,10,1,128]{3,2,1,0:T(1,128)S(1)}, f32[19,10,1,128]{3,2,1,0:T(1,128)S(1)}, u32[]{:S(2)}, u32[]{:S(2)}) collective-permute-start(f32[19,10,1,128]{3,2,1,0:T(1,128)S(1)} %get-tuple-element.375), channel_id=1, source_target_pairs={{0,4},{4,0},{1,5},{5,1},{2,6},{6,2},{3,7},{7,3},{8,12},{12,8},{9,1... | collective-permute-start | bytes 291848 | tf_op jit(solution)/shard_map/ppermute | solution.py:49
  19.8 1.4 %collective-permute-start.3 = (f32[19,10,1,128]{3,2,1,0:T(1,128)S(1)}, f32[19,10,1,128]{3,2,1,0:T(1,128)S(1)}, u32[]{:S(2)}, u32[]{:S(2)}) collective-permute-start(f32[19,10,1,128]{3,2,1,0:T(1,128)S(1)} %get-tuple-element.376), channel_id=1, source_target_pairs={{4,0},{0,4},{5,1},{1,5},{6,2},{2,6},{7,3},{3,7},{12,8},{8,12},{13,... | collective-permute-start | bytes 291848 | tf_op jit(solution)/shard_map/ppermute | solution.py:51
  25.4 4.5 %copy-start.15 = (s32[2,8,128]{2,1,0:T(8,128)S(1)}, s32[2,8,128]{2,1,0:T(8,128)}, u32[]{:S(2)}) copy-start(s32[2,8,128]{2,1,0:T(8,128)} %param.55) | copy-start | bytes 24580
  25.4 5.6 %collective-permute-start.5 = (f32[19,10,10,1]{0,3,2,1:T(1,128)S(1)}, f32[19,10,10,1]{0,3,2,1:T(1,128)S(1)}, u32[]{:S(2)}, u32[]{:S(2)}) collective-permute-start(f32[19,10,10,1]{0,3,2,1:T(1,128)S(1)} %copy.55), channel_id=1, source_target_pairs={{1,0},{2,1},{3,2},{0,3},{5,4},{6,5},{7,6},{4,7},{9,8},{10,9},{11,1... | collective-permute-start | bytes 22808 | tf_op jit(solution)/shard_map/ppermute | solution.py:51
  29.8 5.9 %collective-permute-start.4 = (f32[19,10,10,1]{0,3,2,1:T(1,128)S(1)}, f32[19,10,10,1]{0,3,2,1:T(1,128)S(1)}, u32[]{:S(2)}, u32[]{:S(2)}) collective-permute-start(f32[19,10,10,1]{0,3,2,1:T(1,128)S(1)} %copy.53), channel_id=1, source_target_pairs={{0,1},{1,2},{2,3},{3,0},{4,5},{5,6},{6,7},{7,4},{8,9},{9,10},{10,1... | collective-permute-start | bytes 22808 | tf_op jit(solution)/shard_map/ppermute | solution.py:49
  29.9 11.0 %copy-start.10 = (pred[1,8,128]{2,1,0:T(8,128)(4,1)}, pred[1,8,128]{2,1,0:T(8,128)(4,1)S(1)}, u32[]{:S(2)}) copy-start(pred[1,8,128]{2,1,0:T(8,128)(4,1)S(1)} %get-tuple-element.317) | copy-start | bytes 3076
  39.4 1.4 %copy-start = (f32[19,10,10,1]{3,2,1,0:T(8,128)S(1)}, f32[19,10,10,1]{3,2,1,0:T(8,128)}, u32[]{:S(2)}) copy-start(f32[19,10,10,1]{3,2,1,0:T(8,128)} %copy.54) | copy-start | bytes 22804
  40.9 0.6 copy-start.12
  48.5 5.3 %collective-permute-start.6 = (f32[19,1,8,128]{3,2,1,0:T(8,128)S(1)}, f32[19,1,8,128]{3,2,1,0:T(8,128)S(1)}, u32[]{:S(2)}, u32[]{:S(2)}) collective-permute-start(f32[19,1,8,128]{3,2,1,0:T(8,128)S(1)} %get-tuple-element.382), channel_id=1, source_target_pairs={{0,8},{8,16},{16,24},{24,0},{1,9},{9,17},{17,25},{25,1},{2,10},{10... | collective-permute-start | bytes 233480 | tf_op jit(solution)/shard_map/ppermute | solution.py:49
  50.6 4.4 %collective-permute-start.7 = (f32[19,1,8,128]{3,2,1,0:T(8,128)S(1)}, f32[19,1,8,128]{3,2,1,0:T(8,128)S(1)}, u32[]{:S(2)}, u32[]{:S(2)}) collective-permute-start(f32[19,1,8,128]{3,2,1,0:T(8,128)S(1)} %get-tuple-element.381), channel_id=1, source_target_pairs={{8,0},{16,8},{24,16},{0,24},{9,1},{17,9},{25,17},{1,25},{10,2},{18... | collective-permute-start | bytes 233480 | tf_op jit(solution)/shard_map/ppermute | solution.py:51
  55.2 1.4 %collective-permute-start.8 = (f32[19,10,1,128]{3,2,1,0:T(1,128)S(1)}, f32[19,10,1,128]{3,2,1,0:T(1,128)S(1)}, u32[]{:S(2)}, u32[]{:S(2)}) collective-permute-start(f32[19,10,1,128]{3,2,1,0:T(1,128)S(1)} %get-tuple-element.371), channel_id=1, source_target_pairs={{0,4},{4,0},{1,5},{5,1},{2,6},{6,2},{3,7},{7,3},{8,12},{12,8},{9,1... | collective-permute-start | bytes 291848 | tf_op jit(solution)/shard_map/ppermute | solution.py:49
  55.2 1.4 %collective-permute-start.9 = (f32[19,10,1,128]{3,2,1,0:T(1,128)S(1)}, f32[19,10,1,128]{3,2,1,0:T(1,128)S(1)}, u32[]{:S(2)}, u32[]{:S(2)}) collective-permute-start(f32[19,10,1,128]{3,2,1,0:T(1,128)S(1)} %get-tuple-element.372), channel_id=1, source_target_pairs={{4,0},{0,4},{5,1},{1,5},{6,2},{2,6},{7,3},{3,7},{12,8},{8,12},{13,... | collective-permute-start | bytes 291848 | tf_op jit(solution)/shard_map/ppermute | solution.py:51
  60.8 10.4 %collective-permute-start.10 = (f32[19,10,10,1]{0,3,2,1:T(1,128)S(1)}, f32[19,10,10,1]{0,3,2,1:T(1,128)}, u32[]{:S(2)}, u32[]{:S(2)}) collective-permute-start(f32[19,10,10,1]{0,3,2,1:T(1,128)S(1)} %copy.57), channel_id=1, source_target_pairs={{0,1},{1,2},{2,3},{3,0},{4,5},{5,6},{6,7},{7,4},{8,9},{9,10},{10,1... | collective-permute-start | bytes 22808 | tf_op jit(solution)/shard_map/ppermute | solution.py:49
  61.6 5.8 %collective-permute-start.11 = (f32[19,10,10,1]{0,3,2,1:T(1,128)S(1)}, f32[19,10,10,1]{0,3,2,1:T(1,128)}, u32[]{:S(2)}, u32[]{:S(2)}) collective-permute-start(f32[19,10,10,1]{0,3,2,1:T(1,128)S(1)} %copy.59), channel_id=1, source_target_pairs={{1,0},{2,1},{3,2},{0,3},{5,4},{6,5},{7,6},{4,7},{9,8},{10,9},{11,1... | collective-permute-start | bytes 22808 | tf_op jit(solution)/shard_map/ppermute | solution.py:51
  69.8 0.7 copy-start.13
  71.2 0.6 copy-start.4
  75.3 1.5 %copy-start.1 = (f32[19,10,10,1]{3,2,1,0:T(8,128)S(1)}, f32[19,10,10,1]{3,2,1,0:T(8,128)}, u32[]{:S(2)}) copy-start(f32[19,10,10,1]{3,2,1,0:T(8,128)} %copy.58) | copy-start | bytes 22804
  75.3 1.5 %copy-start.11 = (pred[1,8,128]{2,1,0:T(8,128)(4,1)S(1)}, pred[1,8,128]{2,1,0:T(8,128)(4,1)}, u32[]{:S(2)}) copy-start(pred[1,8,128]{2,1,0:T(8,128)(4,1)} %copy-done.10) | copy-start | bytes 3076
  77.5 1.4 %copy-start.14 = (pred[1,8,128]{2,1,0:T(8,128)(4,1)S(1)}, pred[1,8,128]{2,1,0:T(8,128)(4,1)}, u32[]{:S(2)}) copy-start(pred[1,8,128]{2,1,0:T(8,128)(4,1)} %copy-done.12) | copy-start | bytes 3076
  78.9 1.5 %copy-start.5 = (f32[8,8,128]{2,1,0:T(8,128)S(1)}, f32[8,8,128]{2,1,0:T(8,128)}, u32[]{:S(2)}) copy-start(f32[8,8,128]{2,1,0:T(8,128)} %copy-done.4) | copy-start | bytes 98308
  78.9 1.5 %copy-start.7 = (s32[8,8,128]{2,1,0:T(8,128)S(1)}, s32[8,8,128]{2,1,0:T(8,128)}, u32[]{:S(2)}) copy-start(s32[8,8,128]{2,1,0:T(8,128)} %param.54) | copy-start | bytes 98308
  81.8 21.2 %copy-start.6 = (f32[1,8,8,128]{3,2,1,0:T(8,128)S(1)}, f32[1,8,8,128]{3,2,1,0:T(8,128)}, u32[]{:S(2)}) copy-start(f32[1,8,8,128]{3,2,1,0:T(8,128)} %get-tuple-element.273) | copy-start | bytes 98308
  81.8 21.3 %copy-start.9 = (f32[2,1,2,64]{3,2,1,0:T(2,128)S(1)}, f32[2,1,2,64]{3,2,1,0:T(2,128)}, u32[]{:S(2)}) copy-start(f32[2,1,2,64]{3,2,1,0:T(2,128)} %param.56) | copy-start | bytes 3076
  81.8 21.3 %copy-start.17 = (f32[2,1,2,64]{3,2,1,0:T(2,128)S(1)}, f32[2,1,2,64]{3,2,1,0:T(2,128)}, u32[]{:S(2)}) copy-start(f32[2,1,2,64]{3,2,1,0:T(2,128)} %param.57) | copy-start | bytes 3076
  81.8 21.3 %copy-start.18 = (f32[2,1,2,1]{3,2,1,0:T(2,128)S(1)}, f32[2,1,2,1]{3,2,1,0:T(2,128)}, u32[]{:S(2)}) copy-start(f32[2,1,2,1]{3,2,1,0:T(2,128)} %get-tuple-element.394) | copy-start | bytes 52
  81.8 21.3 %copy-start.19 = (f32[2,1,2,1]{3,2,1,0:T(2,128)S(1)}, f32[2,1,2,1]{3,2,1,0:T(2,128)}, u32[]{:S(2)}) copy-start(f32[2,1,2,1]{3,2,1,0:T(2,128)} %get-tuple-element.395) | copy-start | bytes 52
  81.9 21.3 %copy-start.20 = (f32[2,1,2,63]{3,2,1,0:T(2,128)S(1)}, f32[2,1,2,63]{3,2,1,0:T(2,128)}, u32[]{:S(2)}) copy-start(f32[2,1,2,63]{3,2,1,0:T(2,128)} %get-tuple-element.396) | copy-start | bytes 3028
  81.9 21.3 %copy-start.21 = (f32[2,1,2,63]{3,2,1,0:T(2,128)S(1)}, f32[2,1,2,63]{3,2,1,0:T(2,128)}, u32[]{:S(2)}) copy-start(f32[2,1,2,63]{3,2,1,0:T(2,128)} %get-tuple-element.397) | copy-start | bytes 3028
  81.9 21.3 %copy-start.22 = (f32[2,1,1,64]{3,2,1,0:T(1,128)S(1)}, f32[2,1,1,64]{3,2,1,0:T(1,128)}, u32[]{:S(2)}) copy-start(f32[2,1,1,64]{3,2,1,0:T(1,128)} %get-tuple-element.392) | copy-start | bytes 1540
  81.9 21.3 %copy-start.23 = (f32[2,1,1,64]{3,2,1,0:T(1,128)S(1)}, f32[2,1,1,64]{3,2,1,0:T(1,128)}, u32[]{:S(2)}) copy-start(f32[2,1,1,64]{3,2,1,0:T(1,128)} %get-tuple-element.393) | copy-start | bytes 1540
  81.9 21.3 %copy-start.25 = (f32[2]{0:T(128)S(1)}, f32[2]{0:T(128)}, u32[]{:S(2)}) copy-start(f32[2]{0:T(128)} %constant.557.clone) | copy-start | bytes 28
  81.9 21.3 %copy-start.27 = (f32[2]{0:T(128)S(1)}, f32[2]{0:T(128)}, u32[]{:S(2)}) copy-start(f32[2]{0:T(128)} %constant.558.clone) | copy-start | bytes 28
  81.9 21.3 %copy-start.28 = (f32[2]{0:T(128)S(1)}, f32[2]{0:T(128)}, u32[]{:S(2)}) copy-start(f32[2]{0:T(128)} %constant.555.clone) | copy-start | bytes 28
  81.9 21.3 %copy-start.29 = (f32[2]{0:T(128)S(1)}, f32[2]{0:T(128)}, u32[]{:S(2)}) copy-start(f32[2]{0:T(128)} %constant.556.clone) | copy-start | bytes 28
  103.1 1.5 %copy-start.3 = (f32[19,8,8,128]{3,2,1,0:T(8,128)}, f32[19,8,8,128]{3,2,1,0:T(8,128)S(1)}, u32[]{:S(2)}) copy-start(f32[19,8,8,128]{3,2,1,0:T(8,128)S(1)} %constant_dynamic-update-slice_fusion.38) | copy-start | bytes 1867780
where the time goes:
time: 106 us; the launch traced here: 105 us
  local copies, waits for them, and re-layouts  29.9 us (28%)
  other arithmetic  22.8 us (22%)
  starting transfers between devices  22.4 us (21%)
  blocking collectives  15.5 us (15%)
  waiting for transfers between devices  12.7 us (12%)
  between operations  1.35 us (1%)
    all_gather x1, blocking collectives, body(): coarse_vel = lax.all_gather(across, 'gx', axis=3, tiled=True)  13.6 us
    ppermute x7, starting transfers between devices, extended(): lax.ppermute(head, axis, [((i + 1) % count, i) for i in range(ends)])  11.8 us
    unnamed x35, other arithmetic  10.8 us
    ppermute x7, starting transfers between devices, extended(): lax.ppermute(tail, axis, [(i, (i + 1) % count) for i in range(ends)])  10.6 us
    ppermute x7, waiting for transfers between devices, extended(): lax.ppermute(tail, axis, [(i, (i + 1) % count) for i in range(ends)])  7.47 us
    unnamed x82, local copies, waits for them, and re-layouts  6.83 us
    slice x5, local copies, waits for them, and re-layouts, extended(): head = lax.slice_in_dim(cells, 0, width, axis=dim)  6.35 us
    ppermute x2, local copies, waits for them, and re-layouts, extended(): lax.ppermute(tail, axis, [(i, (i + 1) % count) for i in range(ends)])  6.09 us
  transfers between devices with their start and end apart: 14, of which 11 were waited for; matrix products, arithmetic and copies ran while one was open for 46% of the time, Pallas kernels for 0%

commit v1 on v0

--- a/solution.py
+++ b/solution.py
@@ -38,6 +38,30 @@
 feed_level = (1.0, 0.5)
 
 
+def recast_the_fields(base_x, d0):
+    f_next = list(base_x.shape[1:])
+    f_next[d0] *= base_x.shape[0]
+    return jnp.moveaxis(base_x, 0, d0).reshape(f_next)
+
+
+def change_the_racks(local_values, axis_key):
+    mat_out = lax.axis_index(axis_key)
+    built = lax.axis_size(axis_key)
+    x_next, main = (built, mat_out)
+    n_now, frame_out = (local_values[None], 1)
+    while frame_out < x_next:
+        frames = []
+        for k in range(x_next):
+            frames.append((k, k ^ frame_out))
+        w1 = lax.ppermute(n_now, axis_key, frames)
+        passed = main & frame_out == 0
+        tile_out = jnp.where(passed, n_now, w1)
+        current_value = jnp.where(passed, w1, n_now)
+        n_now = jnp.concatenate([tile_out, current_value])
+        frame_out *= 2
+    return n_now
+
+
 def extended(cells, sides, width, closed):
     for axis, dim in sides:
         count = lax.axis_size(axis)
@@ -156,6 +180,11 @@
 
 
 def body(populations, solid, ports, concentration, loaded):
+
+    def press_patch(row_data, target, dimension_no=3):
+        r_now = change_the_racks(row_data, target)
+        return recast_the_fields(r_now, dimension_no)
+
     depth, height, width = solid.shape
     slab_pos = lax.axis_index("gz")
     first_dev = slab_pos == 0
@@ -182,7 +211,7 @@
     fluid = (solid == 0).astype(jnp.float32)
     local = jnp.stack([block_sum(flow * fluid) for flow in flows]) / (512.0 * base_density)
     across = lax.all_gather(local, "gy", axis=2, tiled=True)
-    coarse_vel = lax.all_gather(across, "gx", axis=3, tiled=True)
+    coarse_vel = press_patch(across, target="gx")
     padded_conc = extended(concentration, (("gz", 1),), 1, False)
     feed = jnp.broadcast_to(
         jnp.array(feed_level, dtype=jnp.float32)[:, None, None],

time: 106 us -> 100 us (0.943)
  blocking collectives: 15.5 us -> 1.83 us
  starting transfers between devices: 22.4 us -> 27.4 us
  waiting for transfers between devices: 12.7 us -> 14.3 us
  local copies, waits for them, and re-layouts: 29.9 us -> 31.3 us
    all_gather x1 -> x0, blocking collectives: 13.6 us -> none  [body(): coarse_vel = lax.all_gather(across, 'gx', axis=3, tiled=True)]
    ppermute x0 -> x2, starting transfers between devices: none -> 4.93 us  [change_the_racks(): w1 = lax.ppermute(n_now, axis_key, frames)]
    ppermute x0 -> x2, waiting for transfers between devices: none -> 1.61 us  [change_the_racks(): w1 = lax.ppermute(n_now, axis_key, frames)]
    unnamed x82 -> x53, local copies, waits for them, and re-layouts: 6.83 us -> 7.22 us
  transfers between devices with their start and end apart: 14 -> 16, of which waited for: 11 -> 12; matrix products, arithmetic and copies ran while one was open for 46% -> 50% of each run, Pallas kernels for 0% -> 0%
where the time goes in v1:
time: 100 us; the launch traced here: 98.8 us
  local copies, waits for them, and re-layouts  31.3 us (31%)
  starting transfers between devices  27.4 us (27%)
  other arithmetic  22.9 us (23%)
  waiting for transfers between devices  14.3 us (14%)
  blocking collectives  1.83 us (2%)
  between operations  1.17 us (1%)
    ppermute x7, starting transfers between devices, extended(): lax.ppermute(head, axis, [((i + 1) % count, i) for i in range(ends)])  11.8 us
    unnamed x35, other arithmetic  10.8 us
    ppermute x7, starting transfers between devices, extended(): lax.ppermute(tail, axis, [(i, (i + 1) % count) for i in range(ends)])  10.6 us
    ppermute x7, waiting for transfers between devices, extended(): lax.ppermute(tail, axis, [(i, (i + 1) % count) for i in range(ends)])  7.51 us
    unnamed x53, local copies, waits for them, and re-layouts  7.22 us
    slice x5, local copies, waits for them, and re-layouts, extended(): head = lax.slice_in_dim(cells, 0, width, axis=dim)  6.36 us
    ppermute x2, local copies, waits for them, and re-layouts, extended(): lax.ppermute(tail, axis, [(i, (i + 1) % count) for i in range(ends)])  6.09 us
    ppermute x7, waiting for transfers between devices, extended(): lax.ppermute(head, axis, [((i + 1) % count, i) for i in range(ends)])  5.19 us
  transfers between devices with their start and end apart: 16, of which 12 were waited for; matrix products, arithmetic and copies ran while one was open for 50% of the time, Pallas kernels for 0%

profile of v1, /device:TPU:0, one launch (start us, length us, event | category | flops | bytes accessed | tf_op | source)
XLA Modules:
  0.0 98.8 jit_solution(11388399996223807255)
XLA Ops:
  0.6 5.5 %collective-permute-start.14 = (f32[2,1,2,64]{3,2,1,0:T(2,128)}, f32[2,1,2,64]{3,2,1,0:T(2,128)}, u32[]{:S(2)}, u32[]{:S(2)}) collective-permute-start(f32[2,1,2,64]{3,2,1,0:T(2,128)} %param.56), channel_id=1, source_target_pairs={{0,8},{8,16},{16,24},{1,9},{9,17},{17,25},{2,10},{10,18},{18,26},{... | collective-permute-start | bytes 3080 | tf_op jit(solution)/shard_map/ppermute | solution.py:73
  6.2 1.3 %collective-permute-start.15 = (f32[2,1,2,64]{3,2,1,0:T(2,128)}, f32[2,1,2,64]{3,2,1,0:T(2,128)}, u32[]{:S(2)}, u32[]{:S(2)}) collective-permute-start(f32[2,1,2,64]{3,2,1,0:T(2,128)} %param.56), channel_id=1, source_target_pairs={{8,0},{16,8},{24,16},{9,1},{17,9},{25,17},{10,2},{18,10},{26,18},{... | collective-permute-start | bytes 3080 | tf_op jit(solution)/shard_map/ppermute | solution.py:75
  7.5 1.2 %constant_dynamic-update-slice_fusion.18 = (f32[19,8,8,128]{3,2,1,0:T(8,128)S(1)}, f32[8,8,128]{2,1,0:T(8,128)S(1)}, f32[8,8,128]{2,1,0:T(8,128)S(1)}, f32[8,8,1...) fusion(f32[19,8,8,128]{3,2,1,0:T(8,128)} %param.53, ...), kind=kLoop, calls=%fused_computation.20 | loop fusion | flops 589823 | bytes 860160
  8.6 0.8 constant_dynamic-update-slice_fusion.17
  9.4 0.8 constant_dynamic-update-slice_fusion.16
  10.3 0.8 constant_dynamic-update-slice_fusion.15
  11.8 2.7 %collective-permute-start = (f32[19,1,8,128]{3,2,1,0:T(8,128)S(1)}, f32[19,1,8,128]{3,2,1,0:T(8,128)S(1)}, u32[]{:S(2)}, u32[]{:S(2)}) collective-permute-start(f32[19,1,8,128]{3,2,1,0:T(8,128)S(1)} %get-tuple-element.383), channel_id=1, source_target_pairs={{0,8},{8,16},{16,24},{24,0},{1,9},{9,17},{17,25},{25,1},{2,10},{10... | collective-permute-start | bytes 233480 | tf_op jit(solution)/shard_map/ppermute | solution.py:73
  14.5 1.1 %collective-permute-start.1 = (f32[19,1,8,128]{3,2,1,0:T(8,128)S(1)}, f32[19,1,8,128]{3,2,1,0:T(8,128)S(1)}, u32[]{:S(2)}, u32[]{:S(2)}) collective-permute-start(f32[19,1,8,128]{3,2,1,0:T(8,128)S(1)} %get-tuple-element.384), channel_id=1, source_target_pairs={{8,0},{16,8},{24,16},{0,24},{9,1},{17,9},{25,17},{1,25},{10,2},{18... | collective-permute-start | bytes 233480 | tf_op jit(solution)/shard_map/ppermute | solution.py:75
  16.2 2.4 %collective-permute-done = f32[19,1,8,128]{3,2,1,0:T(8,128)S(1)} collective-permute-done((f32[19,1,8,128]{3,2,1,0:T(8,128)S(1)}, f32[19,1,8,128]{3,2,1,0:T(8,128)S(1)}, u32[]{:S(2)}, u32[]{:S(2)}) %collective-permute-start) | collective-permute-done | bytes 77856 | tf_op jit(solution)/shard_map/ppermute | solution.py:73
  18.6 0.9 collective-permute-done.1
  21.5 1.7 %fusion.392 = (f32[19,10,10,1]{3,2,1,0:T(8,128)}, f32[19,10,10,1]{3,2,1,0:T(8,128)S(1)}) fusion(f32[19,10,10,128]{3,2,1,0:T(8,128)S(1)} %pad_maximum_fusion), kind=kLoop, calls=%fused_computation.688 | loop fusion | bytes 30400 | tf_op jit(solution)/shard_map/slice | solution.py:69
  23.2 2.1 %copy.69 = f32[19,10,10,1]{0,3,2,1:T(1,128)S(1)} copy(f32[19,10,10,1]{3,2,1,0:T(8,128)} %get-tuple-element.355) | data formatting | bytes 15200 | tf_op jit(solution)/shard_map/slice | solution.py:69
  25.4 3.6 %collective-permute-start.5 = (f32[19,10,10,1]{0,3,2,1:T(1,128)S(1)}, f32[19,10,10,1]{0,3,2,1:T(1,128)S(1)}, u32[]{:S(2)}, u32[]{:S(2)}) collective-permute-start(f32[19,10,10,1]{0,3,2,1:T(1,128)S(1)} %copy.69), channel_id=1, source_target_pairs={{1,0},{2,1},{3,2},{0,3},{5,4},{6,5},{7,6},{4,7},{9,8},{10,9},{11,1... | collective-permute-start | bytes 22808 | tf_op jit(solution)/shard_map/ppermute | solution.py:75
  29.0 0.8 copy.67
  29.9 1.0 %collective-permute-done.5 = f32[19,10,10,1]{0,3,2,1:T(1,128)S(1)} collective-permute-done((f32[19,10,10,1]{0,3,2,1:T(1,128)S(1)}, f32[19,10,10,1]{0,3,2,1:T(1,128)S(1)}, u32[]{:S(2)}, u32[]{:S(2)}) %collective-permute-start.5) | collective-permute-done | bytes 7632 | tf_op jit(solution)/shard_map/ppermute | solution.py:75
  31.0 1.6 %copy.70 = f32[19,10,10,1]{3,2,1,0:T(8,128)S(1)} copy(f32[19,10,10,1]{0,3,2,1:T(1,128)S(1)} %collective-permute-done.5) | data formatting | bytes 15200 | tf_op jit(solution)/shard_map/ppermute | solution.py:75
  32.7 3.0 %collective-permute-done.4 = f32[19,10,10,1]{0,3,2,1:T(1,128)S(1)} collective-permute-done((f32[19,10,10,1]{0,3,2,1:T(1,128)S(1)}, f32[19,10,10,1]{0,3,2,1:T(1,128)S(1)}, u32[]{:S(2)}, u32[]{:S(2)}) %collective-permute-start.4) | collective-permute-done | bytes 7632 | tf_op jit(solution)/shard_map/ppermute | solution.py:73
  35.7 2.7 %copy.68 = f32[19,10,10,1]{3,2,1,0:T(8,128)} copy(f32[19,10,10,1]{0,3,2,1:T(1,128)S(1)} %collective-permute-done.4) | data formatting | bytes 15200 | tf_op jit(solution)/shard_map/ppermute | solution.py:73
  38.4 1.0 maximum_bitcast_fusion.13
  39.5 1.3 %copy-done = f32[19,10,10,1]{3,2,1,0:T(8,128)S(1)} copy-done((f32[19,10,10,1]{3,2,1,0:T(8,128)S(1)}, f32[19,10,10,1]{3,2,1,0:T(8,128)}, u32[]{:S(2)}) %copy-start) | copy-done | bytes 7624
  48.5 2.1 %collective-permute-start.6 = (f32[19,1,8,128]{3,2,1,0:T(8,128)S(1)}, f32[19,1,8,128]{3,2,1,0:T(8,128)S(1)}, u32[]{:S(2)}, u32[]{:S(2)}) collective-permute-start(f32[19,1,8,128]{3,2,1,0:T(8,128)S(1)} %get-tuple-element.382), channel_id=1, source_target_pairs={{0,8},{8,16},{16,24},{24,0},{1,9},{9,17},{17,25},{25,1},{2,10},{10... | collective-permute-start | bytes 233480 | tf_op jit(solution)/shard_map/ppermute | solution.py:73
  50.6 0.8 collective-permute-start.7
  52.1 1.7 %collective-permute-done.6 = f32[19,1,8,128]{3,2,1,0:T(8,128)S(1)} collective-permute-done((f32[19,1,8,128]{3,2,1,0:T(8,128)S(1)}, f32[19,1,8,128]{3,2,1,0:T(8,128)S(1)}, u32[]{:S(2)}, u32[]{:S(2)}) %collective-permute-start.6) | collective-permute-done | bytes 77856 | tf_op jit(solution)/shard_map/ppermute | solution.py:73
  53.8 1.2 %collective-permute-done.7 = f32[19,1,8,128]{3,2,1,0:T(8,128)S(1)} collective-permute-done((f32[19,1,8,128]{3,2,1,0:T(8,128)S(1)}, f32[19,1,8,128]{3,2,1,0:T(8,128)S(1)}, u32[]{:S(2)}, u32[]{:S(2)}) %collective-permute-start.7) | collective-permute-done | bytes 77856 | tf_op jit(solution)/shard_map/ppermute | solution.py:75
  57.0 1.7 %fusion.391 = (f32[19,10,10,1]{3,2,1,0:T(8,128)S(1)}, f32[19,10,10,1]{3,2,1,0:T(8,128)}) fusion(f32[19,10,10,128]{3,2,1,0:T(8,128)S(1)} %pad_maximum_fusion.1), kind=kLoop, calls=%fused_computation.687 | loop fusion | bytes 30400 | tf_op jit(solution)/shard_map/slice | solution.py:69
  58.7 2.1 %copy.71 = f32[19,10,10,1]{0,3,2,1:T(1,128)S(1)} copy(f32[19,10,10,1]{3,2,1,0:T(8,128)} %get-tuple-element.354) | data formatting | bytes 15200 | tf_op jit(solution)/shard_map/slice | solution.py:70
  60.9 0.8 copy.73
  61.7 4.0 %collective-permute-start.11 = (f32[19,10,10,1]{0,3,2,1:T(1,128)S(1)}, f32[19,10,10,1]{0,3,2,1:T(1,128)}, u32[]{:S(2)}, u32[]{:S(2)}) collective-permute-start(f32[19,10,10,1]{0,3,2,1:T(1,128)S(1)} %copy.73), channel_id=1, source_target_pairs={{1,0},{2,1},{3,2},{0,3},{5,4},{6,5},{7,6},{4,7},{9,8},{10,9},{11,1... | collective-permute-start | bytes 22808 | tf_op jit(solution)/shard_map/ppermute | solution.py:75
  65.7 1.7 %collective-permute-done.11 = f32[19,10,10,1]{0,3,2,1:T(1,128)} collective-permute-done((f32[19,10,10,1]{0,3,2,1:T(1,128)S(1)}, f32[19,10,10,1]{0,3,2,1:T(1,128)}, u32[]{:S(2)}, u32[]{:S(2)}) %collective-permute-start.11) | collective-permute-done | bytes 7632 | tf_op jit(solution)/shard_map/ppermute | solution.py:75
  67.5 2.4 %copy.74 = f32[19,10,10,1]{3,2,1,0:T(8,128)S(1)} copy(f32[19,10,10,1]{0,3,2,1:T(1,128)} %collective-permute-done.11) | data formatting | bytes 15200 | tf_op jit(solution)/shard_map/ppermute | solution.py:75
  71.9 3.4 %copy.72 = f32[19,10,10,1]{3,2,1,0:T(8,128)} copy(f32[19,10,10,1]{0,3,2,1:T(1,128)} %collective-permute-done.10) | data formatting | bytes 15200 | tf_op jit(solution)/shard_map/ppermute | solution.py:73
  75.3 1.1 %maximum_bitcast_fusion.3 = (f32[8,8,128]{2,1,0:T(8,128)S(1)}, f32[8,8,128]{2,1,0:T(8,128)S(1)}, f32[8,8,128]{2,1,0:T(8,128)S(1)}) fusion(f32[19,10,10,1]{3,2,1,0:T(8,128)} %copy.72, f32[19,10,1,128]{3,2,1,0:T(1,128)S(1)} %collective-permute-done.9, f32[19,10,1,128]{3,2,1,0:T(1,128)S(1)} %collective-permute-done.8, ...), kind=kLoop, calls=%fused_computation.399 | loop fusion | flops 106496 | bytes 1078704 | tf_op jit(solution)/shard_map/squeeze | solution.py:201
  76.8 0.8 constant_dynamic-update-slice_fusion.57
  78.2 0.7 constant_dynamic-update-slice_fusion.59
  79.0 0.8 constant_dynamic-update-slice_fusion.60
  79.7 0.7 constant_dynamic-update-slice_fusion.63
  80.5 1.4 %select_reduce_fusion = (f32[128]{0:T(128)}, f32[128]{0:T(128)}, f32[128]{0:T(128)}, f32[1,8,8,128]{3,2,1,0:T(8,128)S(1)}, f32[1,8,8,128]{3,2,1,0:T(8,128)S(1)},...) fusion(f32[8,8,128]{2,1,0:T(8,128)S(1)} %get-tuple-element.278,, ...), kind=kLoop, calls=%fused_computation.509 | loop fusion | flops 573056 | bytes 1612128 | tf_op jit(solution)/shard_map/reduce_sum | solution.py:151
  81.9 0.7 reduce_sum.37
  82.6 0.7 reduce_sum.40
  84.4 1.8 %all_gather.3 = f32[3,1,2,16]{3,1,0,2:T(1,128)S(1)} all-gather(f32[3,1,1,16]{3,1,0,2:T(1,128)S(1)} %fusion.364), channel_id=1, replica_groups=mesh['gz'=4,'gy'=2,'gx'=4] {'gy'}, dimensions={2}, use_global_device_ids=true | all-gather | bytes 576 | tf_op jit(solution)/shard_map/all_gather | solution.py:213
  86.3 0.8 constant_dynamic-update-slice_fusion.53
  87.1 0.8 constant_dynamic-update-slice_fusion.52
  87.9 0.8 constant_dynamic-update-slice_fusion.51
  88.6 0.8 constant_dynamic-update-slice_fusion.50
  89.5 0.8 constant_dynamic-update-slice_fusion.41
  90.3 4.8 %collective-permute-start.13 = (f32[2,3,1,2,16]{4,0,3,2,1:T(2,128)S(1)}, f32[2,3,1,2,16]{4,0,3,2,1:T(2,128)S(1)}, u32[]{:S(2)}, u32[]{:S(2)}) collective-permute-start(f32[2,3,1,2,16]{4,0,3,2,1:T(2,128)S(1)} %pad_maximum_fusion.38), channel_id=1, source_target_pairs={{0,2},{1,3},{2,0},{3,1},{4,6},{5,7},{6,4},{7,5},{8,10},{9,11},{10,... | collective-permute-start | bytes 2312 | tf_op jit(solution)/shard_map/ppermute | solution.py:56
  95.1 1.6 %collective-permute-done.13 = f32[2,3,1,2,16]{4,0,3,2,1:T(2,128)S(1)} collective-permute-done((f32[2,3,1,2,16]{4,0,3,2,1:T(2,128)S(1)}, f32[2,3,1,2,16]{4,0,3,2,1:T(2,128)S(1)}, u32[]{:S(2)}, u32[]{:S(2)}) %collective-permute-start.13) | collective-permute-done | bytes 800 | tf_op jit(solution)/shard_map/ppermute | solution.py:56
  97.4 1.4 %multiply_subtract_fusion = f32[2,1,2,64]{3,2,1,0:T(2,128)} fusion(f32[2,1,2,64]{3,2,1,0:T(2,128)S(1)} %copy-done.8, f32[2,1,2,1]{3,2,1,0:T(2,128)} %get-tuple-element.403, f32[2,1,2,63]{3,2,1,0:T(2,128)} %get-tuple-element.405, f32[2,1,2,63]{3,2,1,0:T(2,128)} %get-tuple-element.404, f32[2,1,2,1]{3,2,1,0:T(2,128)} %get-tuple-element.402, ...), kind=kLoop, calls=%fused_computation.682 | loop fusion | flops 10496 | bytes 11810 | tf_op jit(solution)/shard_map/sub | solution.py:178
  (138 shorter events, 18.7 us)
Async XLA Ops:
  0.6 10.4 %copy-start.2 = (f32[19,8,8,128]{3,2,1,0:T(8,128)S(1)}, f32[19,8,8,128]{3,2,1,0:T(8,128)}, u32[]{:S(2)}) copy-start(f32[19,8,8,128]{3,2,1,0:T(8,128)} %param.53) | copy-start | bytes 1867780
  0.6 96.7 %collective-permute-start.14 = (f32[2,1,2,64]{3,2,1,0:T(2,128)}, f32[2,1,2,64]{3,2,1,0:T(2,128)}, u32[]{:S(2)}, u32[]{:S(2)}) collective-permute-start(f32[2,1,2,64]{3,2,1,0:T(2,128)} %param.56), channel_id=1, source_target_pairs={{0,8},{8,16},{16,24},{1,9},{9,17},{17,25},{2,10},{10,18},{18,26},{... | collective-permute-start | bytes 3080 | tf_op jit(solution)/shard_map/ppermute | solution.py:73
  6.2 91.2 %collective-permute-start.15 = (f32[2,1,2,64]{3,2,1,0:T(2,128)}, f32[2,1,2,64]{3,2,1,0:T(2,128)}, u32[]{:S(2)}, u32[]{:S(2)}) collective-permute-start(f32[2,1,2,64]{3,2,1,0:T(2,128)} %param.56), channel_id=1, source_target_pairs={{8,0},{16,8},{24,16},{9,1},{17,9},{25,17},{10,2},{18,10},{26,18},{... | collective-permute-start | bytes 3080 | tf_op jit(solution)/shard_map/ppermute | solution.py:75
  11.2 4.3 %copy-start.7 = (f32[2,1,2,64]{3,2,1,0:T(2,128)S(1)}, f32[2,1,2,64]{3,2,1,0:T(2,128)}, u32[]{:S(2)}) copy-start(f32[2,1,2,64]{3,2,1,0:T(2,128)} %param.56) | copy-start | bytes 3076
  11.3 4.3 %copy-start.14 = (f32[2,1,2,64]{3,2,1,0:T(2,128)S(1)}, f32[2,1,2,64]{3,2,1,0:T(2,128)}, u32[]{:S(2)}) copy-start(f32[2,1,2,64]{3,2,1,0:T(2,128)} %param.57) | copy-start | bytes 3076
  11.3 4.3 %copy-start.15 = (f32[2]{0:T(128)S(1)}, f32[2]{0:T(128)}, u32[]{:S(2)}) copy-start(f32[2]{0:T(128)} %constant.562.clone) | copy-start | bytes 28
  11.3 4.3 %copy-start.16 = (f32[2]{0:T(128)S(1)}, f32[2]{0:T(128)}, u32[]{:S(2)}) copy-start(f32[2]{0:T(128)} %constant.563.clone) | copy-start | bytes 28
  11.8 6.9 %collective-permute-start = (f32[19,1,8,128]{3,2,1,0:T(8,128)S(1)}, f32[19,1,8,128]{3,2,1,0:T(8,128)S(1)}, u32[]{:S(2)}, u32[]{:S(2)}) collective-permute-start(f32[19,1,8,128]{3,2,1,0:T(8,128)S(1)} %get-tuple-element.383), channel_id=1, source_target_pairs={{0,8},{8,16},{16,24},{24,0},{1,9},{9,17},{17,25},{25,1},{2,10},{10... | collective-permute-start | bytes 233480 | tf_op jit(solution)/shard_map/ppermute | solution.py:73
  14.5 5.1 %collective-permute-start.1 = (f32[19,1,8,128]{3,2,1,0:T(8,128)S(1)}, f32[19,1,8,128]{3,2,1,0:T(8,128)S(1)}, u32[]{:S(2)}, u32[]{:S(2)}) collective-permute-start(f32[19,1,8,128]{3,2,1,0:T(8,128)S(1)} %get-tuple-element.384), channel_id=1, source_target_pairs={{8,0},{16,8},{24,16},{0,24},{9,1},{17,9},{25,17},{1,25},{10,2},{18... | collective-permute-start | bytes 233480 | tf_op jit(solution)/shard_map/ppermute | solution.py:75
  19.7 1.4 %collective-permute-start.2 = (f32[19,10,1,128]{3,2,1,0:T(1,128)S(1)}, f32[19,10,1,128]{3,2,1,0:T(1,128)S(1)}, u32[]{:S(2)}, u32[]{:S(2)}) collective-permute-start(f32[19,10,1,128]{3,2,1,0:T(1,128)S(1)} %get-tuple-element.375), channel_id=1, source_target_pairs={{0,4},{4,0},{1,5},{5,1},{2,6},{6,2},{3,7},{7,3},{8,12},{12,8},{9,1... | collective-permute-start | bytes 291848 | tf_op jit(solution)/shard_map/ppermute | solution.py:73
  19.8 1.4 %collective-permute-start.3 = (f32[19,10,1,128]{3,2,1,0:T(1,128)S(1)}, f32[19,10,1,128]{3,2,1,0:T(1,128)S(1)}, u32[]{:S(2)}, u32[]{:S(2)}) collective-permute-start(f32[19,10,1,128]{3,2,1,0:T(1,128)S(1)} %get-tuple-element.376), channel_id=1, source_target_pairs={{4,0},{0,4},{5,1},{1,5},{6,2},{2,6},{7,3},{3,7},{12,8},{8,12},{13,... | collective-permute-start | bytes 291848 | tf_op jit(solution)/shard_map/ppermute | solution.py:75
  25.4 4.5 %copy-start.13 = (s32[2,8,128]{2,1,0:T(8,128)S(1)}, s32[2,8,128]{2,1,0:T(8,128)}, u32[]{:S(2)}) copy-start(s32[2,8,128]{2,1,0:T(8,128)} %param.55) | copy-start | bytes 24580
  25.4 5.6 %collective-permute-start.5 = (f32[19,10,10,1]{0,3,2,1:T(1,128)S(1)}, f32[19,10,10,1]{0,3,2,1:T(1,128)S(1)}, u32[]{:S(2)}, u32[]{:S(2)}) collective-permute-start(f32[19,10,10,1]{0,3,2,1:T(1,128)S(1)} %copy.69), channel_id=1, source_target_pairs={{1,0},{2,1},{3,2},{0,3},{5,4},{6,5},{7,6},{4,7},{9,8},{10,9},{11,1... | collective-permute-start | bytes 22808 | tf_op jit(solution)/shard_map/ppermute | solution.py:75
  29.8 5.9 %collective-permute-start.4 = (f32[19,10,10,1]{0,3,2,1:T(1,128)S(1)}, f32[19,10,10,1]{0,3,2,1:T(1,128)S(1)}, u32[]{:S(2)}, u32[]{:S(2)}) collective-permute-start(f32[19,10,10,1]{0,3,2,1:T(1,128)S(1)} %copy.67), channel_id=1, source_target_pairs={{0,1},{1,2},{2,3},{3,0},{4,5},{5,6},{6,7},{7,4},{8,9},{9,10},{10,1... | collective-permute-start | bytes 22808 | tf_op jit(solution)/shard_map/ppermute | solution.py:73
  29.9 11.0 %copy-start.9 = (pred[1,8,128]{2,1,0:T(8,128)(4,1)}, pred[1,8,128]{2,1,0:T(8,128)(4,1)S(1)}, u32[]{:S(2)}) copy-start(pred[1,8,128]{2,1,0:T(8,128)(4,1)S(1)} %get-tuple-element.317) | copy-start | bytes 3076
  39.4 1.4 %copy-start = (f32[19,10,10,1]{3,2,1,0:T(8,128)S(1)}, f32[19,10,10,1]{3,2,1,0:T(8,128)}, u32[]{:S(2)}) copy-start(f32[19,10,10,1]{3,2,1,0:T(8,128)} %copy.68) | copy-start | bytes 22804
  40.9 0.6 copy-start.11
  48.5 5.3 %collective-permute-start.6 = (f32[19,1,8,128]{3,2,1,0:T(8,128)S(1)}, f32[19,1,8,128]{3,2,1,0:T(8,128)S(1)}, u32[]{:S(2)}, u32[]{:S(2)}) collective-permute-start(f32[19,1,8,128]{3,2,1,0:T(8,128)S(1)} %get-tuple-element.382), channel_id=1, source_target_pairs={{0,8},{8,16},{16,24},{24,0},{1,9},{9,17},{17,25},{25,1},{2,10},{10... | collective-permute-start | bytes 233480 | tf_op jit(solution)/shard_map/ppermute | solution.py:73
  50.6 4.4 %collective-permute-start.7 = (f32[19,1,8,128]{3,2,1,0:T(8,128)S(1)}, f32[19,1,8,128]{3,2,1,0:T(8,128)S(1)}, u32[]{:S(2)}, u32[]{:S(2)}) collective-permute-start(f32[19,1,8,128]{3,2,1,0:T(8,128)S(1)} %get-tuple-element.381), channel_id=1, source_target_pairs={{8,0},{16,8},{24,16},{0,24},{9,1},{17,9},{25,17},{1,25},{10,2},{18... | collective-permute-start | bytes 233480 | tf_op jit(solution)/shard_map/ppermute | solution.py:75
  55.2 1.4 %collective-permute-start.8 = (f32[19,10,1,128]{3,2,1,0:T(1,128)S(1)}, f32[19,10,1,128]{3,2,1,0:T(1,128)S(1)}, u32[]{:S(2)}, u32[]{:S(2)}) collective-permute-start(f32[19,10,1,128]{3,2,1,0:T(1,128)S(1)} %get-tuple-element.371), channel_id=1, source_target_pairs={{0,4},{4,0},{1,5},{5,1},{2,6},{6,2},{3,7},{7,3},{8,12},{12,8},{9,1... | collective-permute-start | bytes 291848 | tf_op jit(solution)/shard_map/ppermute | solution.py:73
  55.2 1.4 %collective-permute-start.9 = (f32[19,10,1,128]{3,2,1,0:T(1,128)S(1)}, f32[19,10,1,128]{3,2,1,0:T(1,128)S(1)}, u32[]{:S(2)}, u32[]{:S(2)}) collective-permute-start(f32[19,10,1,128]{3,2,1,0:T(1,128)S(1)} %get-tuple-element.372), channel_id=1, source_target_pairs={{4,0},{0,4},{5,1},{1,5},{6,2},{2,6},{7,3},{3,7},{12,8},{8,12},{13,... | collective-permute-start | bytes 291848 | tf_op jit(solution)/shard_map/ppermute | solution.py:75
  60.8 10.4 %collective-permute-start.10 = (f32[19,10,10,1]{0,3,2,1:T(1,128)S(1)}, f32[19,10,10,1]{0,3,2,1:T(1,128)}, u32[]{:S(2)}, u32[]{:S(2)}) collective-permute-start(f32[19,10,10,1]{0,3,2,1:T(1,128)S(1)} %copy.71), channel_id=1, source_target_pairs={{0,1},{1,2},{2,3},{3,0},{4,5},{5,6},{6,7},{7,4},{8,9},{9,10},{10,1... | collective-permute-start | bytes 22808 | tf_op jit(solution)/shard_map/ppermute | solution.py:73
  61.7 5.8 %collective-permute-start.11 = (f32[19,10,10,1]{0,3,2,1:T(1,128)S(1)}, f32[19,10,10,1]{0,3,2,1:T(1,128)}, u32[]{:S(2)}, u32[]{:S(2)}) collective-permute-start(f32[19,10,10,1]{0,3,2,1:T(1,128)S(1)} %copy.73), channel_id=1, source_target_pairs={{1,0},{2,1},{3,2},{0,3},{5,4},{6,5},{7,6},{4,7},{9,8},{10,9},{11,1... | collective-permute-start | bytes 22808 | tf_op jit(solution)/shard_map/ppermute | solution.py:75
  69.9 0.7 copy-start.12
  71.3 0.6 copy-start.4
  75.3 1.5 %copy-start.1 = (f32[19,10,10,1]{3,2,1,0:T(8,128)S(1)}, f32[19,10,10,1]{3,2,1,0:T(8,128)}, u32[]{:S(2)}) copy-start(f32[19,10,10,1]{3,2,1,0:T(8,128)} %copy.72) | copy-start | bytes 22804
  75.3 1.5 %copy-start.10 = (pred[1,8,128]{2,1,0:T(8,128)(4,1)S(1)}, pred[1,8,128]{2,1,0:T(8,128)(4,1)}, u32[]{:S(2)}) copy-start(pred[1,8,128]{2,1,0:T(8,128)(4,1)} %copy-done.9) | copy-start | bytes 3076
  79.0 1.5 %copy-start.5 = (f32[8,8,128]{2,1,0:T(8,128)S(1)}, f32[8,8,128]{2,1,0:T(8,128)}, u32[]{:S(2)}) copy-start(f32[8,8,128]{2,1,0:T(8,128)} %copy-done.4) | copy-start | bytes 98308
  79.0 1.5 %copy-start.6 = (s32[8,8,128]{2,1,0:T(8,128)S(1)}, s32[8,8,128]{2,1,0:T(8,128)}, u32[]{:S(2)}) copy-start(s32[8,8,128]{2,1,0:T(8,128)} %param.54) | copy-start | bytes 98308
  80.5 16.9 %copy-start.8 = (f32[2,1,2,64]{3,2,1,0:T(2,128)S(1)}, f32[2,1,2,64]{3,2,1,0:T(2,128)}, u32[]{:S(2)}) copy-start(f32[2,1,2,64]{3,2,1,0:T(2,128)} %param.56) | copy-start | bytes 3076
  86.2 4.0 %collective-permute-start.12 = (f32[1,3,1,2,16]{4,0,3,2,1:T(1,128)S(1)}, f32[1,3,1,2,16]{4,0,3,2,1:T(1,128)S(1)}, u32[]{:S(2)}, u32[]{:S(2)}) collective-permute-start(f32[1,3,1,2,16]{4,0,3,2,1:T(1,128)S(1)} %bitcast.625), channel_id=1, source_target_pairs={{0,1},{1,0},{2,3},{3,2},{4,5},{5,4},{6,7},{7,6},{8,9},{9,8},{10,11... | collective-permute-start | bytes 1160 | tf_op jit(solution)/shard_map/ppermute | solution.py:56
  90.3 6.4 %collective-permute-start.13 = (f32[2,3,1,2,16]{4,0,3,2,1:T(2,128)S(1)}, f32[2,3,1,2,16]{4,0,3,2,1:T(2,128)S(1)}, u32[]{:S(2)}, u32[]{:S(2)}) collective-permute-start(f32[2,3,1,2,16]{4,0,3,2,1:T(2,128)S(1)} %pad_maximum_fusion.38), channel_id=1, source_target_pairs={{0,2},{1,3},{2,0},{3,1},{4,6},{5,7},{6,4},{7,5},{8,10},{9,11},{10,... | collective-permute-start | bytes 2312 | tf_op jit(solution)/shard_map/ppermute | solution.py:56
  95.1 3.7 %copy-start.3 = (f32[19,8,8,128]{3,2,1,0:T(8,128)}, f32[19,8,8,128]{3,2,1,0:T(8,128)S(1)}, u32[]{:S(2)}) copy-start(f32[19,8,8,128]{3,2,1,0:T(8,128)S(1)} %constant_dynamic-update-slice_fusion.38) | copy-start | bytes 1867780
